TPU v7x, 32 devices: a whole 2x2x4 slice. The times are simulated.
32 devices in a mesh: row: 8 (over z, y), col: 4 (over x, core).
Axes of the slice: x: 2, y: 2, z: 4, core: 2. Of those that a mesh axis runs over, the one named last changes fastest.
Arguments:
- grad_window: float32 [4096, 7168], P('row', 'col'), may hold values from -6 to 6
- rows_first: float32 [4096, 256], P('row'), may hold values from -0.09375 to 0.09375
- cols_first: float32 [7168, 256], P('col'), may hold values from -0.0625 to 0.0625
- rows_second: float32 [4096, 256], P('row'), may hold values from -0.09375 to 0.09375
- cols_second: float32 [7168, 256], P('col'), may hold values from -0.0625 to 0.0625
- inverse_first: float32 [256, 256], replicated, may hold values from -2 to 2, as said below
- inverse_second: float32 [256, 256], replicated, may hold values from -2 to 2, as said below
Outputs:
- panel_second: float32 [4096, 256], P('row')
- pivot_second: float32 [7168, 256], P('col')
- panel_first: float32 [4096, 256], P('row')
- pivot_first: float32 [7168, 256], P('col')
Inputs may be any that keep to these rules, and one draw needn't show every extreme that they name: `inverse_first`: lower triangular, diagonal entries between 1 and 2. `inverse_second`: lower triangular, diagonal entries between 1 and 2.
All inputs are finite; a program needn't handle non-finite values.
Results may differ from a plain program's by a relative error of at most 0.000071.
Values sent between devices are 32-bit elements; how exact they have to be, the bound alone decides.
A program may use at most 64 MiB of HBM per device.

v0:
```python
import jax
import jax.numpy as jnp
from jax import lax
from jax.sharding import PartitionSpec as P


def from_root(array, axis, root):
    mine = lax.axis_index(axis) == root
    return lax.psum(jnp.where(mine, array, jnp.zeros_like(array)), axis)


def matmul(left, right):
    return jnp.dot(left, right, precision=lax.Precision.HIGHEST, preferred_element_type=jnp.float32)


def tmatmul(left, right):
    return lax.dot_general(
        left,
        right,
        (((0,), (0,)), ((), ())),
        precision=lax.Precision.HIGHEST,
        preferred_element_type=jnp.float32,
    )


def local(
    grad_window, rows_first, cols_first, rows_second, cols_second, inverse_first, inverse_second
):
    col_count = lax.axis_size("col")
    is_last = lax.axis_index("col") == col_count - 1
    tile_cols = grad_window.shape[1]
    width = inverse_first.shape[0]
    corner = from_root(cols_first[tile_cols - width :], "col", col_count - 1)
    sum_second, sum_first = lax.psum(
        (matmul(grad_window, cols_second), matmul(grad_window, cols_first)), "col"
    )
    panel_second = matmul(-sum_second, inverse_second)
    panel_first = matmul(-(sum_first + matmul(panel_second, corner)), inverse_first)
    pivot_two, pivot_one = lax.psum(
        (tmatmul(grad_window, rows_second), tmatmul(grad_window, rows_first)), "row"
    )
    extra = lax.psum(tmatmul(panel_second, rows_first), "row")
    pivot_second = matmul(-pivot_two, inverse_second)
    pivot_one = pivot_one.at[tile_cols - width :].add(jnp.where(is_last, extra, 0.0))
    pivot_first = matmul(-pivot_one, inverse_first)
    return (panel_second, pivot_second, panel_first, pivot_first)


def solution(mesh):
    in_specs = (
        P("row", "col"),
        P("row", None),
        P("col", None),
        P("row", None),
        P("col", None),
        P(),
        P(),
    )
    out_specs = (P("row", None), P("col", None), P("row", None), P("col", None))
    return jax.shard_map(local, mesh=mesh, in_specs=in_specs, out_specs=out_specs, check_vma=False)
```

profile of v0, /device:TPU:0, one launch (start us, length us, event | category | flops | bytes accessed | tf_op | source)
XLA Modules:
  0.0 229.8 jit_solution(15416958554598284297)
XLA Ops:
  7.2 0.0 copy-start
  7.2 0.0 all-reduce.7.cloned.1.call-start
  7.2 1.8 slice_select_fusion
  9.0 6.6 %fusion.10 = f32[512,256]{1,0:T(8,128)} fusion(f32[512,1792]{1,0:T(8,128)} %param.9, f32[1792,256]{1,0:T(8,128)} %param.11), kind=kOutput, calls=%fused_computation.13 | convolution fusion | flops 2818572288 | bytes 6029312 | tf_op jit(solution)/shard_map/dot_general | solution.py:13
  15.6 0.0 copy-done
  15.6 0.0 copy-done.1
  15.6 3.8 %fusion.8 = f32[512,256]{1,0:T(8,128)} fusion(f32[512,1792]{1,0:T(8,128)S(1)} %copy-done.1, f32[1792,256]{1,0:T(8,128)S(1)} %copy-done), kind=kOutput, calls=%fused_computation.11 | convolution fusion | flops 2818572288 | bytes 6029312 | tf_op jit(solution)/shard_map/dot_general | solution.py:13
  19.5 0.0 all-reduce.7.cloned.1.call-update
  19.5 0.0 copy-start.5
  19.5 0.2 all-reduce.5.cloned.1.call-start
  19.7 0.0 copy-done.8
  19.7 0.0 copy-start.2
  19.8 9.3 %fusion.9 = f32[1792,256]{1,0:T(8,128)} fusion(f32[512,1792]{1,0:T(8,128)} %param.9, f32[512,256]{1,0:T(8,128)S(1)} %copy-done.8), kind=kOutput, calls=%fused_computation.12 | convolution fusion | flops 2818572288 | bytes 6029312 | tf_op jit(solution)/shard_map/dot_general | solution.py:17
  29.1 0.0 copy-done.5
  29.1 0.0 copy-done.2
  29.1 7.4 %fusion.12 = f32[1792,256]{1,0:T(8,128)} fusion(f32[512,1792]{1,0:T(8,128)S(1)} %copy-done.2, f32[512,256]{1,0:T(8,128)S(1)} %copy-done.5), kind=kOutput, calls=%fused_computation.15 | convolution fusion | flops 2818572288 | bytes 6029312 | tf_op jit(solution)/shard_map/dot_general | solution.py:17
  36.5 25.2 %all-reduce.7.cloned.1.call-done = (f32[512,256]{1,0:T(8,128)}, f32[512,256]{1,0:T(8,128)}, f32[256,256]{1,0:T(8,128)}) async-done(((f32[512,256]{1,0:T(8,128)}, f32[512,256]{1,0:T(8,128)}, f32[256,256]{1,0:T(8,128)}), (f32[512,256]{1,0:T(8,128)}, f32[512,256]{1,0:T(8,128)}, f32[256,256]{1,0:T(8,128)})) %all-reduce.7.cloned.1.call-update) | async-done | bytes 1310736 | tf_op jit(solution)/shard_map/psum | solution.py:34
  61.6 0.0 copy-done.6
  61.6 1.9 fusion.5
  63.5 0.0 copy-start.3
  63.5 1.7 fusion.13
  65.2 0.0 all-reduce.5.cloned.1.call-update
  65.3 0.0 copy-start.7
  65.3 0.0 copy-done.3
  65.3 1.0 copy-done.9
  66.3 1.5 fusion.4
  67.8 1.4 fusion.11
  69.2 146.3 %all-reduce.5.cloned.1.call-done = (f32[1792,256]{1,0:T(8,128)}, f32[1792,256]{1,0:T(8,128)}, f32[256,256]{1,0:T(8,128)}) async-done(((f32[1792,256]{1,0:T(8,128)}, f32[1792,256]{1,0:T(8,128)}, f32[256,256]{1,0:T(8,128)}), (f32[1792,256]{1,0:T(8,128)}, f32[1792,256]{1,0:T(8,128)}, f32[256,256]{1,0:T(8,128)})) %all-reduce.5.cloned.1.call-update) | async-done | bytes 3932176 | tf_op jit(solution)/shard_map/psum | solution.py:39
  215.5 4.5 %fusion.2 = f32[1792,256]{1,0:T(8,128)} fusion(f32[256,256]{1,0:T(8,128)S(1)} %copy-done.6, f32[1792,256]{1,0:T(8,128)} %get-tuple-element.16), kind=kOutput, calls=%fused_computation.2 | convolution fusion | flops 1409744896 | bytes 3932160 | tf_op jit(solution)/shard_map/dot_general | solution.py:13
  220.0 0.0 copy-done.4
  220.0 0.1 fusion.7
  220.1 2.8 %fusion = f32[1792,256]{1,0:T(8,128)} fusion(f32[256,256]{1,0:T(8,128)S(1)} %copy-done.7, f32[1792,256]{1,0:T(8,128)S(1)} %fusion.7), kind=kOutput, calls=%fused_computation | convolution fusion | flops 1409744896 | bytes 3932160 | tf_op jit(solution)/shard_map/dot_general | solution.py:13
  (8 shorter events, 0.0 us)
Async XLA Ops:
  7.2 8.5 %copy-start = (f32[1792,256]{1,0:T(8,128)S(1)}, f32[1792,256]{1,0:T(8,128)}, u32[]{:S(2)}) copy-start(f32[1792,256]{1,0:T(8,128)} %param.13) | copy-start | bytes 5505028
  7.2 54.4 %all-reduce.7.cloned.1.call-start = ((), (), s32[]{:S(2)}) async-start(), calls=%async_computation.1 | async-start | bytes 2621440 | tf_op jit(solution)/shard_map/psum | solution.py:34
  9.0 6.6 %copy-start.1 = (f32[512,1792]{1,0:T(8,128)S(1)}, f32[512,1792]{1,0:T(8,128)}, u32[]{:S(2)}) copy-start(f32[512,1792]{1,0:T(8,128)} %param.9) | copy-start | bytes 11010052
  15.6 4.1 %copy-start.8 = (f32[512,256]{1,0:T(8,128)S(1)}, f32[512,256]{1,0:T(8,128)}, u32[]{:S(2)}) copy-start(f32[512,256]{1,0:T(8,128)} %param.12) | copy-start | bytes 1572868
  19.5 9.6 %copy-start.5 = (f32[512,256]{1,0:T(8,128)S(1)}, f32[512,256]{1,0:T(8,128)}, u32[]{:S(2)}) copy-start(f32[512,256]{1,0:T(8,128)} %param.10) | copy-start | bytes 1572868
  19.5 196.0 %all-reduce.5.cloned.1.call-start = ((), (), s32[]{:S(2)}) async-start(), calls=%async_computation | async-start | bytes 7864320 | tf_op jit(solution)/shard_map/psum | solution.py:39
  19.7 9.3 %copy-start.2 = (f32[512,1792]{1,0:T(8,128)S(1)}, f32[512,1792]{1,0:T(8,128)}, u32[]{:S(2)}) copy-start(f32[512,1792]{1,0:T(8,128)} %param.9) | copy-start | bytes 11010052
  29.1 32.6 %copy-start.6 = (f32[256,256]{1,0:T(8,128)S(1)}, f32[256,256]{1,0:T(8,128)}, u32[]{:S(2)}) copy-start(f32[256,256]{1,0:T(8,128)} %param.15) | copy-start | bytes 786436
  63.5 1.8 copy-start.3
  65.2 1.0 copy-start.9
  65.3 2.6 %copy-start.7 = (f32[256,256]{1,0:T(8,128)S(1)}, f32[256,256]{1,0:T(8,128)}, u32[]{:S(2)}) copy-start(f32[256,256]{1,0:T(8,128)} %param.14) | copy-start | bytes 786436
  215.5 4.5 %copy-start.4 = (f32[1792,256]{1,0:T(8,128)S(1)}, f32[1792,256]{1,0:T(8,128)}, u32[]{:S(2)}) copy-start(f32[1792,256]{1,0:T(8,128)} %get-tuple-element.17) | copy-start | bytes 5505028
  215.5 4.5 %copy-start.10 = (f32[256,256]{1,0:T(8,128)S(1)}, f32[256,256]{1,0:T(8,128)}, u32[]{:S(2)}) copy-start(f32[256,256]{1,0:T(8,128)} %get-tuple-element.18) | copy-start | bytes 786436
Sparse Core Ops, SparseCore 0:
  19.6 41.9 all-reduce.6
  66.0 149.4 all-reduce.4
where the time goes:
time: 230 us
  waiting for transfers between devices  172 us (75%)
  matrix products  40.9 us (18%)
  between operations  14.1 us (6%)
    psum x1, waiting for transfers between devices, local(): lax.psum((tmatmul(grad_window, rows_second), tmatmul(grad_window, rows_fi...  146 us
    psum x1, waiting for transfers between devices, local(): lax.psum((matmul(grad_window, cols_second), matmul(grad_window, cols_firs...  25.2 us
    dot_general x7, matrix products, matmul(): jnp.dot(left, right, precision=lax.Precision.HIGHEST, preferred_element_t...  22.5 us
    dot_general x3, matrix products, tmatmul(): lax.dot_general(left, right, (((0,), (0,)), ((), ())), precision=lax.Prec...  18.4 us
  transfers between devices with their start and end apart: 2, of which 2 were waited for; matrix products, arithmetic and copies ran while one was open for 9% of the time, Pallas kernels for 0%

commit v1 on v0

v1 whole, which is shorter than its diff:
```python
import functools

import jax
import jax.numpy as jnp
from jax import lax
from jax.experimental import pallas as pl
from jax.experimental.pallas import tpu as pltpu
from jax.sharding import PartitionSpec as P

MESH = pl.DeviceIdType.MESH
F32 = jnp.float32
BLOCK = 256


def split(x):
    high = x.astype(jnp.bfloat16)
    return high, (x - high.astype(F32)).astype(jnp.bfloat16)


def dot3(a, b):
    (ah, al), (bh, bl) = a, b
    out = jnp.dot(ah, bh, preferred_element_type=F32)
    out += jnp.dot(ah, bl, preferred_element_type=F32)
    return out + jnp.dot(al, bh, preferred_element_type=F32)


def kernel(
    n, m,
    g_hbm, r1_hbm, c1_hbm, r2_hbm, c2_hbm, i1_hbm, i2_hbm,
    panel2_hbm, pivot2_hbm, panel1_hbm, pivot1_hbm,
    g, rows, cols, inv, part, slot, pivot, left, gathered, panel,
    load_sem, ring_send, ring_recv, col_send, col_recv, out_sem, panel_sem,
):
    height, width = g.shape
    nb = inv.shape[-1]
    blocks = width // BLOCK
    chunk = width // n
    half = chunk // 2
    piece = height // m

    row = lax.axis_index("row")
    col = lax.axis_index("col")
    pos = row // 2 + (row % 2) * (n - 1 - 2 * (row // 2))

    def at_position(p):
        p = p % n
        back = p // (n // 2)
        return (1 - back) * 2 * p + back * (2 * n - 2 * p - 1)

    following, preceding = at_position(pos + 1), at_position(pos + n - 1)

    sources = (g_hbm, r2_hbm, c2_hbm, i2_hbm, r1_hbm, c1_hbm, i1_hbm)
    targets = (g, rows.at[0], cols.at[0], inv.at[0], rows.at[1], cols.at[1], inv.at[1])
    loads = [
        pltpu.make_async_copy(s, t, load_sem.at[k]) for k, (s, t) in enumerate(zip(sources, targets))
    ]
    for load in loads:
        load.start()

    barrier = pltpu.get_barrier_semaphore()
    for peer in (following, preceding):
        pl.semaphore_signal(barrier, inc=1, device_id={"row": peer}, device_id_type=MESH)
    for k in range(1, m):
        pl.semaphore_signal(barrier, inc=1, device_id={"col": (col + k) % m}, device_id_type=MESH)
    pl.semaphore_wait(barrier, m + 1)

    pending = []

    def rows_of(index, way):
        return pl.ds(pl.multiple_of((index % n) * chunk + way * half, 8), half)

    def ring_copy(kind, way, step):
        flow = 2 * kind + way
        sign = 1 - 2 * way
        if step < n - 1:
            if step == 0:
                source = part.at[kind, rows_of(pos, way)]
            else:
                source = slot.at[flow, step - 1]
            target = slot.at[flow, step]
        else:
            where = rows_of(pos + n + sign * (1 - (step - n + 1)) + n, way)
            source = pivot.at[kind, where]
            target = pivot.at[kind, where]
        return pltpu.make_async_remote_copy(
            src_ref=source,
            dst_ref=target,
            send_sem=ring_send.at[flow, step],
            recv_sem=ring_recv.at[flow, step],
            device_id={"row": following if way == 0 else preceding},
            device_id_type=MESH,
        )

    outs = (pivot2_hbm, pivot1_hbm)

    def put(kind, way, index):
        flow = 2 * kind + way
        where = rows_of(index, way)
        copy = pltpu.make_async_copy(pivot.at[kind, where], outs[kind].at[where], out_sem.at[flow])
        copy.start()

    def ring_send_step(kind, step):
        for way in range(2):
            copy = ring_copy(kind, way, step)
            copy.start()
            pending.append(copy)

    def ring_step(kind, step):
        for way in range(2):
            flow = 2 * kind + way
            sign = 1 - 2 * way
            ring_copy(kind, way, step).wait_recv()
            if step < n - 1:
                index = pos + 2 * n - sign * (step + 1)
                where = rows_of(index, way)
                total = slot[flow, step] + part[kind, where, :]
                if step < n - 2:
                    slot[flow, step] = total
                else:
                    pivot[kind, where, :] = -dot3(split(total), split(inv[kind]))
            else:
                index = pos + 2 * n - sign * (step - n + 1)
            if step < 2 * n - 3:
                copy = ring_copy(kind, way, step + 1)
                copy.start()
                pending.append(copy)
            if step >= n - 2:
                put(kind, way, index)

    def products(kind):
        @pl.loop(0, blocks)
        def _(k):
            where = pl.ds(pl.multiple_of(k * BLOCK, BLOCK), BLOCK)
            part[kind, where, :] = dot3(split(g[:, where].T), split(rows[kind]))

    def lefts(kind):
        left[...] = jnp.zeros_like(left)

        @pl.loop(0, blocks)
        def _(k):
            where = pl.ds(pl.multiple_of(k * BLOCK, BLOCK), BLOCK)
            left[...] += dot3(split(g[:, where]), split(cols[kind, where, :]))

    def piece_of(index):
        return pl.ds(pl.multiple_of(index * piece, 8), piece)

    def scatter_copy(kind, k):
        return pltpu.make_async_remote_copy(
            src_ref=left.at[piece_of((col + k) % m)],
            dst_ref=gathered.at[kind, k - 1],
            send_sem=col_send.at[kind, 0, k - 1],
            recv_sem=col_recv.at[kind, 0, k - 1],
            device_id={"col": (col + k) % m},
            device_id_type=MESH,
        )

    def gather_copy(kind, k):
        mine = piece_of(col)
        return pltpu.make_async_remote_copy(
            src_ref=panel.at[kind, mine],
            dst_ref=panel.at[kind, mine],
            send_sem=col_send.at[kind, 1, k - 1],
            recv_sem=col_recv.at[kind, 1, k - 1],
            device_id={"col": (col + k) % m},
            device_id_type=MESH,
        )

    def col_scatter(kind):
        for k in range(1, m):
            scatter_copy(kind, k).start()

    def col_gather(kind):
        total = left[piece_of(col), :]
        for k in range(1, m):
            scatter_copy(kind, k).wait_recv()
            total += gathered[kind, k - 1]
        panel[kind, piece_of(col), :] = -dot3(split(total), split(inv[kind]))
        for k in range(1, m):
            gather_copy(kind, k).start()
        for k in range(1, m):
            scatter_copy(kind, k).wait_send()

    panels = (panel2_hbm, panel1_hbm)

    def put_panel(kind):
        return pltpu.make_async_copy(panel.at[kind], panels[kind], panel_sem.at[kind])

    def col_finish(kind):
        for k in range(1, m):
            gather_copy(kind, k).wait_recv()
        put_panel(kind).start()

    loads[0].wait()
    loads[1].wait()
    products(0)
    ring_send_step(0, 0)
    loads[2].wait()
    lefts(0)
    col_scatter(0)
    ring_step(0, 0)
    loads[3].wait()
    col_gather(0)
    ring_step(0, 1)
    col_finish(0)

    @pl.when(col == m - 1)
    def _():
        g[:, width - nb :] += panel[0]

    loads[4].wait()
    products(1)
    ring_send_step(1, 0)
    loads[5].wait()
    lefts(1)
    loads[6].wait()
    col_scatter(1)
    steps = 2 * n - 2
    for step in range(2, steps + 2):
        if step < steps:
            ring_step(0, step)
        ring_step(1, step - 2)
        if step == 4:
            col_gather(1)
        if step == 7:
            col_finish(1)

    for copy in pending:
        copy.wait_send()
    for kind in range(2):
        for k in range(1, m):
            gather_copy(kind, k).wait_send()
        put_panel(kind).wait()
        for way in range(2):
            for _ in range(n):
                where = pl.ds(way * half, half)
                pltpu.make_async_copy(
                    pivot.at[kind, where], outs[kind].at[where], out_sem.at[2 * kind + way]
                ).wait()


def solution(mesh):
    n, m = mesh.shape["row"], mesh.shape["col"]

    def local(g, r1, c1, r2, c2, i1, i2):
        height, width = g.shape
        nb = i1.shape[0]
        half = width // n // 2
        any_space = pl.BlockSpec(memory_space=pl.ANY)
        tall = jax.ShapeDtypeStruct((height, nb), F32)
        wide = jax.ShapeDtypeStruct((width, nb), F32)
        steps = 2 * n - 2
        return pl.pallas_call(
            functools.partial(kernel, n, m),
            out_shape=(tall, wide, tall, wide),
            in_specs=[any_space] * 7,
            out_specs=(any_space,) * 4,
            scratch_shapes=[
                pltpu.VMEM((height, width), F32),
                pltpu.VMEM((2, height, nb), F32),
                pltpu.VMEM((2, width, nb), F32),
                pltpu.VMEM((2, nb, nb), F32),
                pltpu.VMEM((2, width, nb), F32),
                pltpu.VMEM((4, n - 1, half, nb), F32),
                pltpu.VMEM((2, width, nb), F32),
                pltpu.VMEM((height, nb), F32),
                pltpu.VMEM((2, m - 1, height // m, nb), F32),
                pltpu.VMEM((2, height, nb), F32),
                pltpu.SemaphoreType.DMA((7,)),
                pltpu.SemaphoreType.DMA((4, steps)),
                pltpu.SemaphoreType.DMA((4, steps)),
                pltpu.SemaphoreType.DMA((2, 2, m - 1)),
                pltpu.SemaphoreType.DMA((2, 2, m - 1)),
                pltpu.SemaphoreType.DMA((4,)),
                pltpu.SemaphoreType.DMA((2,)),
            ],
            compiler_params=pltpu.CompilerParams(collective_id=0, has_side_effects=True),
        )(g, r1, c1, r2, c2, i1, i2)

    return jax.shard_map(
        local,
        mesh=mesh,
        in_specs=(P("row", "col"), P("row", None), P("col", None), P("row", None), P("col", None), P(), P()),
        out_specs=(P("row", None), P("col", None), P("row", None), P("col", None)),
        check_vma=False,
    )
```

time: 230 us -> 105 us (0.46)
  waiting for transfers between devices: 172 us -> 0 us
  Pallas kernels: 0 us -> 97.1 us
  matrix products: 40.9 us -> 0 us
  between operations: 14.1 us -> 0.64 us
  local copies, waits for them, and re-layouts: 1.05 us -> 6.89 us
    psum x2 -> x0, waiting for transfers between devices: 172 us -> none  [the longest x1 146 us: local(): lax.psum((tmatmul(grad_window, rows_second), tmatmul(grad_window, rows_fi...]
    pallas_call x0 -> x1, Pallas kernels: none -> 97.1 us  [local(): pl.pallas_call(functools.partial(kernel, n, m), out_shape=(tall, wide, ta...]
    dot_general x10 -> x0, matrix products: 40.9 us -> none  [the longest x7 22.5 us: matmul(): jnp.dot(left, right, precision=lax.Precision.HIGHEST, preferred_element_t...]
    unnamed x22 -> x8, local copies, waits for them, and re-layouts: 1.05 us -> 6.89 us
  transfers between devices with their start and end apart: 2 -> 0, of which waited for: 2 -> 0; matrix products, arithmetic and copies ran while one was open for 9% -> 0% of each run, Pallas kernels for 0% -> 0%
where the time goes in v1:
time: 105 us
  Pallas kernels  97.1 us (92%)
  local copies, waits for them, and re-layouts  6.89 us (7%)
    pallas_call x1, Pallas kernels, local(): pl.pallas_call(functools.partial(kernel, n, m), out_shape=(tall, wide, ta...  97.1 us
    unnamed x8, local copies, waits for them, and re-layouts  6.89 us

profile of v1, /device:TPU:0, one launch (start us, length us, event | category | flops | bytes accessed | tf_op | source)
XLA Modules:
  0.0 104.6 jit_solution(7120836833771369526)
XLA Ops:
  0.6 97.1 %shard_map.102 = (f32[512,256]{1,0:T(8,128)}, f32[1792,256]{1,0:T(8,128)}, f32[512,256]{1,0:T(8,128)}, f32[1792,256]{1,0:T(8,128)}) custom-call(f32[512,1792]{1,0:T(8,128)} %g_hbm.1, f32[512,256]{1,0:T(8,128)} %r1_hbm.1, f32[1792,256]{1,0:T(8,128)} %c1_hbm.1, f32[512,256]{1,0:T(8,128)} %r2_hbm.1, f32[1792,256]{1,0:T(8,128)} %c2_hbm.1, f32[256,256]{1,0:T(8,128)} %i1_hbm.1, ...), custom_call_target="tpu_custom_call" | custom-call | tf_op jit(solution)/shard_map/pallas_call | solution.py:252
  97.7 1.9 %copy.15 = f32[512,256]{1,0:T(8,128)} copy(f32[512,256]{1,0:T(8,128)} %get-tuple-element.8) | data formatting | bytes 1048576
  99.6 0.0 copy-start.1
  99.6 0.0 copy-start
  99.6 3.0 %copy.16 = f32[1792,256]{1,0:T(8,128)} copy(f32[1792,256]{1,0:T(8,128)} %get-tuple-element.9) | data formatting | bytes 3670016
  102.6 0.0 copy-done.1
  102.6 0.8 copy.17
  103.4 0.0 copy-done
  103.4 1.2 %copy.18 = f32[1792,256]{1,0:T(8,128)} copy(f32[1792,256]{1,0:T(8,128)S(1)} %copy-done) | data formatting | bytes 3670016
Async XLA Ops:
  99.6 3.0 %copy-start.1 = (f32[512,256]{1,0:T(8,128)S(1)}, f32[512,256]{1,0:T(8,128)}, u32[]{:S(2)}) copy-start(f32[512,256]{1,0:T(8,128)} %get-tuple-element.10) | copy-start | bytes 1572868
  99.6 3.8 %copy-start = (f32[1792,256]{1,0:T(8,128)S(1)}, f32[1792,256]{1,0:T(8,128)}, u32[]{:S(2)}) copy-start(f32[1792,256]{1,0:T(8,128)} %get-tuple-element.11) | copy-start | bytes 5505028

commit v2 on v1

v2 whole, which is shorter than its diff:
```python
import functools

import jax
import jax.numpy as jnp
from jax import lax
from jax.experimental import pallas as pl
from jax.experimental.pallas import tpu as pltpu
from jax.sharding import PartitionSpec as P

MESH = pl.DeviceIdType.MESH
F32 = jnp.float32
BLOCK = 256
LATE = 5
VMEM_LIMIT = 48 << 20


def split(x):
    high = x.astype(jnp.bfloat16)
    return high, (x - high.astype(F32)).astype(jnp.bfloat16)


def dot3(a, b):
    (ah, al), (bh, bl) = a, b
    out = jnp.dot(ah, bh, preferred_element_type=F32)
    out += jnp.dot(ah, bl, preferred_element_type=F32)
    return out + jnp.dot(al, bh, preferred_element_type=F32)


def kernel(
    n, m,
    g_hbm, r1_hbm, c1_hbm, r2_hbm, c2_hbm, i1_hbm, i2_hbm,
    panel2, pivot2, panel1, pivot1,
    g, rows, cols, inv, part, slot2, slot1, slot_late, left, gathered,
    load_sem, ring_send, ring_recv, col_send, col_recv,
):
    height, width = g.shape
    nb = inv.shape[-1]
    blocks = width // BLOCK
    piece = height // m
    early = width - nb

    row = lax.axis_index("row")
    col = lax.axis_index("col")
    pos = row // 2 + (row % 2) * (n - 1 - 2 * (row // 2))

    def at_position(p):
        p = p % n
        back = p // (n // 2)
        return (1 - back) * 2 * p + back * (2 * n - 2 * p - 1)

    following, preceding = at_position(pos + 1), at_position(pos + n - 1)

    sources = (g_hbm, r2_hbm, r1_hbm, c2_hbm, i2_hbm, c1_hbm, i1_hbm)
    targets = (g, rows.at[0], rows.at[1], cols.at[0], inv.at[0], cols.at[1], inv.at[1])
    loads = [
        pltpu.make_async_copy(s, t, load_sem.at[k]) for k, (s, t) in enumerate(zip(sources, targets))
    ]
    for load in loads:
        load.start()

    barrier = pltpu.get_barrier_semaphore()
    for peer in (following, preceding):
        pl.semaphore_signal(barrier, inc=1, device_id={"row": peer}, device_id_type=MESH)
    for k in range(1, m):
        pl.semaphore_signal(barrier, inc=1, device_id={"col": (col + k) % m}, device_id_type=MESH)

    pending = []

    groups = ((0, 0, width, slot2), (1, 0, early, slot1), (1, early, nb, slot_late))
    pivots = (pivot2, pivot1)
    panels = (panel2, panel1)

    def rows_of(group, index, way):
        _, base, span, _ = groups[group]
        chunk = span // n
        half = chunk // 2
        return pl.ds(pl.multiple_of(base + (index % n) * chunk + way * half, 8), half)

    def ring_copy(group, way, step):
        kind, _, _, slot = groups[group]
        sign = 1 - 2 * way
        if step < n - 1:
            if step == 0:
                source = part.at[kind, rows_of(group, pos, way)]
            else:
                source = slot.at[way, step - 1]
            target = slot.at[way, step]
        else:
            where = rows_of(group, pos + 2 * n + sign * (1 - (step - n + 1)), way)
            source = pivots[kind].at[where]
            target = pivots[kind].at[where]
        return pltpu.make_async_remote_copy(
            src_ref=source,
            dst_ref=target,
            send_sem=ring_send.at[group, way, step],
            recv_sem=ring_recv.at[group, way, step],
            device_id={"row": following if way == 0 else preceding},
            device_id_type=MESH,
        )

    def ring_start(group):
        for way in range(2):
            copy = ring_copy(group, way, 0)
            copy.start()
            pending.append(copy)

    def ring_step(group, step):
        kind, _, _, slot = groups[group]
        for way in range(2):
            sign = 1 - 2 * way
            ring_copy(group, way, step).wait_recv()
            if step < n - 1:
                where = rows_of(group, pos + 2 * n - sign * (step + 1), way)
                total = slot[way, step] + part[kind, where, :]
                if step < n - 2:
                    slot[way, step] = total
                else:
                    pivots[kind][where, :] = -dot3(split(total), split(inv[kind]))
            if step < 2 * n - 3:
                copy = ring_copy(group, way, step + 1)
                copy.start()
                pending.append(copy)

    def block_of(k):
        return pl.ds(pl.multiple_of(k * BLOCK, BLOCK), BLOCK)

    def products(kind, first, last):
        @pl.loop(first, last)
        def _(k):
            part[kind, block_of(k), :] = dot3(split(g[:, block_of(k)].T), split(rows[kind]))

    def lefts(kind, first, last):
        @pl.loop(first, last)
        def _(k):
            left[kind] += dot3(split(g[:, block_of(k)]), split(cols[kind, block_of(k), :]))

    def piece_of(index):
        return pl.ds(pl.multiple_of(index * piece, 8), piece)

    def scatter_copy(kind, k):
        return pltpu.make_async_remote_copy(
            src_ref=left.at[kind, piece_of((col + k) % m)],
            dst_ref=gathered.at[kind, k - 1],
            send_sem=col_send.at[kind, 0, k - 1],
            recv_sem=col_recv.at[kind, 0, k - 1],
            device_id={"col": (col + k) % m},
            device_id_type=MESH,
        )

    def gather_copy(kind, k):
        mine = piece_of(col)
        return pltpu.make_async_remote_copy(
            src_ref=panels[kind].at[mine],
            dst_ref=panels[kind].at[mine],
            send_sem=col_send.at[kind, 1, k - 1],
            recv_sem=col_recv.at[kind, 1, k - 1],
            device_id={"col": (col + k) % m},
            device_id_type=MESH,
        )

    def col_scatter(kind):
        for k in range(1, m):
            scatter_copy(kind, k).start()

    def col_gather(kind):
        total = left[kind, piece_of(col), :]
        for k in range(1, m):
            scatter_copy(kind, k).wait_recv()
            total += gathered[kind, k - 1]
        panels[kind][piece_of(col), :] = -dot3(split(total), split(inv[kind]))
        for k in range(1, m):
            gather_copy(kind, k).start()

    def col_finish(kind):
        for k in range(1, m):
            gather_copy(kind, k).wait_recv()

    left[...] = jnp.zeros_like(left)
    last_block = early // BLOCK
    loads[0].wait()
    loads[1].wait()
    products(0, 0, blocks)
    pl.semaphore_wait(barrier, m + 1)
    ring_start(0)
    loads[2].wait()
    products(1, 0, last_block)
    ring_start(1)
    loads[3].wait()
    lefts(0, 0, blocks)
    col_scatter(0)
    for load in loads[4:]:
        load.wait()
    steps = 2 * n - 2
    late = 0
    for step in range(steps):
        if step >= LATE:
            for _ in range(2):
                if late < steps:
                    ring_step(2, late)
                    late += 1
                if _ == 0:
                    ring_step(0, step)
                else:
                    ring_step(1, step)
        else:
            ring_step(0, step)
            ring_step(1, step)
        if step < 3:
            lefts(1, step * last_block // 3, (step + 1) * last_block // 3)
        if step == 2:
            col_gather(0)
        if step == LATE - 1:
            col_finish(0)

            @pl.when(col == m - 1)
            def _():
                g[:, early:] += panel2[...]

            products(1, last_block, blocks)
            ring_start(2)
            lefts(1, last_block, blocks)
            col_scatter(1)
        if step == LATE + 2:
            col_gather(1)
    while late < steps:
        ring_step(2, late)
        late += 1
    col_finish(1)

    for copy in pending:
        copy.wait_send()
    for kind in range(2):
        for k in range(1, m):
            scatter_copy(kind, k).wait_send()
            gather_copy(kind, k).wait_send()


def write_out(*refs):
    sems = refs[-1]
    copies = [pltpu.make_async_copy(refs[k], refs[4 + k], sems.at[k]) for k in range(4)]
    for copy in copies:
        copy.start()
    for copy in copies:
        copy.wait()


def solution(mesh):
    n, m = mesh.shape["row"], mesh.shape["col"]

    def local(g, r1, c1, r2, c2, i1, i2):
        height, width = g.shape
        nb = i1.shape[0]
        any_space = pl.BlockSpec(memory_space=pl.ANY)
        vmem = pl.BlockSpec(memory_space=pltpu.VMEM)
        shapes = ((height, nb), (width, nb), (height, nb), (width, nb))
        steps = 2 * n - 2
        results = pl.pallas_call(
            functools.partial(kernel, n, m),
            out_shape=tuple(pltpu.VMEM(s, F32) for s in shapes),
            in_specs=[pl.BlockSpec(memory_space=pltpu.HBM)] * 7,
            out_specs=(vmem,) * 4,
            scratch_shapes=[
                pltpu.VMEM((height, width), F32),
                pltpu.VMEM((2, height, nb), F32),
                pltpu.VMEM((2, width, nb), F32),
                pltpu.VMEM((2, nb, nb), F32),
                pltpu.VMEM((2, width, nb), F32),
                pltpu.VMEM((2, n - 1, width // n // 2, nb), F32),
                pltpu.VMEM((2, n - 1, (width - nb) // n // 2, nb), F32),
                pltpu.VMEM((2, n - 1, nb // n // 2, nb), F32),
                pltpu.VMEM((2, height, nb), F32),
                pltpu.VMEM((2, m - 1, height // m, nb), F32),
                pltpu.SemaphoreType.DMA((7,)),
                pltpu.SemaphoreType.DMA((3, 2, steps)),
                pltpu.SemaphoreType.DMA((3, 2, steps)),
                pltpu.SemaphoreType.DMA((2, 2, m - 1)),
                pltpu.SemaphoreType.DMA((2, 2, m - 1)),
            ],
            compiler_params=pltpu.CompilerParams(
                collective_id=0, has_side_effects=True, vmem_limit_bytes=VMEM_LIMIT
            ),
        )(g, r1, c1, r2, c2, i1, i2)
        return pl.pallas_call(
            write_out,
            out_shape=tuple(jax.ShapeDtypeStruct(s, F32) for s in shapes),
            in_specs=[vmem] * 4,
            out_specs=(any_space,) * 4,
            scratch_shapes=[pltpu.SemaphoreType.DMA((4,))],
            compiler_params=pltpu.CompilerParams(vmem_limit_bytes=8 << 20),
        )(*results)

    return jax.shard_map(
        local,
        mesh=mesh,
        in_specs=(P("row", "col"), P("row", None), P("col", None), P("row", None), P("col", None), P(), P()),
        out_specs=(P("row", None), P("col", None), P("row", None), P("col", None)),
        check_vma=False,
    )
```

time: 105 us -> 93.3 us (0.89)
  Pallas kernels: 97.1 us -> 89.5 us
  local copies, waits for them, and re-layouts: 6.89 us -> 2.93 us
    pallas_call x1 -> x2, Pallas kernels: 97.1 us -> 89.5 us  [the longest x1 87.3 us: local(): pl.pallas_call(functools.partial(kernel, n, m), out_shape=tuple((pltpu.VM...]
    unnamed x8 -> x6, local copies, waits for them, and re-layouts: 6.89 us -> 2.93 us
where the time goes in v2:
time: 93.3 us; the launch traced here: 93.1 us
  Pallas kernels  89.5 us (96%)
  local copies, waits for them, and re-layouts  2.93 us (3%)
    pallas_call x1, Pallas kernels, local(): pl.pallas_call(functools.partial(kernel, n, m), out_shape=tuple((pltpu.VM...  87.3 us
    unnamed x6, local copies, waits for them, and re-layouts  2.93 us
    pallas_call x1, Pallas kernels, local(): pl.pallas_call(write_out, out_shape=tuple((jax.ShapeDtypeStruct(s, F32) f...  2.21 us

profile of v2, /device:TPU:0, one launch (start us, length us, event | category | flops | bytes accessed | tf_op | source)
XLA Modules:
  0.0 93.1 jit_solution(9655483761119441438)
XLA Ops:
  0.6 0.0 copy-start
  0.6 1.0 %copy-done = f32[512,256]{1,0:T(8,128)S(1)} copy-done((f32[512,256]{1,0:T(8,128)S(1)}, f32[512,256]{1,0:T(8,128)}, u32[]{:S(2)}) %copy-start) | copy-done | bytes 524312
  1.7 0.0 copy-start.1
  1.7 0.9 %copy-done.1 = f32[256,256]{1,0:T(8,128)S(1)} copy-done((f32[256,256]{1,0:T(8,128)S(1)}, f32[256,256]{1,0:T(8,128)}, u32[]{:S(2)}) %copy-start.1) | copy-done | bytes 262168
  2.6 0.0 copy-start.2
  2.6 0.9 %copy-done.2 = f32[256,256]{1,0:T(8,128)S(1)} copy-done((f32[256,256]{1,0:T(8,128)S(1)}, f32[256,256]{1,0:T(8,128)}, u32[]{:S(2)}) %copy-start.2) | copy-done | bytes 262168
  3.6 87.3 %shard_map.102 = (f32[512,256]{1,0:T(8,128)S(1)}, f32[1792,256]{1,0:T(8,128)S(1)}, f32[512,256]{1,0:T(8,128)S(1)}, f32[1792,256]{1,0:T(8,128)S(1)}) custom-call(f32[512,1792]{1,0:T(8,128)} %g_hbm.1, f32[512,256]{1,0:T(8,128)S(1)} %copy-done, f32[1792,256]{1,0:T(8,128)} %c1_hbm.1, f32[512,256]{1,0:T(8,128)} %r2_hbm.1, f32[1792,256]{1,0:T(8,128)} %c2_hbm.1, ...), custom_call_target="tpu_custom_call" | custom-call | tf_op jit(solution)/shard_map/pallas_call | solution.py:257
  90.9 2.2 %shard_map.103 = (f32[512,256]{1,0:T(8,128)}, f32[1792,256]{1,0:T(8,128)}, f32[512,256]{1,0:T(8,128)}, f32[1792,256]{1,0:T(8,128)}) custom-call(f32[512,256]{1,0:T(8,128)S(1)} %get-tuple-element.8.refs_0_, f32[1792,256]{1,0:T(8,128)S(1)} %get-tuple-element.9.refs_1_, f32[512,256]{1,0:T(8,128)S(1)} %get-tuple-element.10.refs_2_, ...), custom_call_target="tpu_custom_call" | custom-call | tf_op jit(solution)/shard_map/pallas_call | solution.py:283
Async XLA Ops:
  0.6 1.0 %copy-start = (f32[512,256]{1,0:T(8,128)S(1)}, f32[512,256]{1,0:T(8,128)}, u32[]{:S(2)}) copy-start(f32[512,256]{1,0:T(8,128)} %r1_hbm.1) | copy-start | bytes 1572868
  1.7 0.9 %copy-start.1 = (f32[256,256]{1,0:T(8,128)S(1)}, f32[256,256]{1,0:T(8,128)}, u32[]{:S(2)}) copy-start(f32[256,256]{1,0:T(8,128)} %i1_hbm.1) | copy-start | bytes 786436
  2.6 0.9 %copy-start.2 = (f32[256,256]{1,0:T(8,128)S(1)}, f32[256,256]{1,0:T(8,128)}, u32[]{:S(2)}) copy-start(f32[256,256]{1,0:T(8,128)} %i2_hbm.1) | copy-start | bytes 786436

commit v3 on v2

--- a/solution.py
+++ b/solution.py
@@ -66,18 +66,23 @@
 
     pending = []
 
-    groups = ((0, 0, width, slot2), (1, 0, early, slot1), (1, early, nb, slot_late))
+    parts = slot2.shape[0]
+    groups = []
+    for q in range(parts):
+        groups += [(0, 0, width, parts, q, slot2.at[q]), (1, 0, early, parts, q, slot1.at[q])]
+    groups.append((1, early, nb, 1, 0, slot_late))
+    late_group = 2 * parts
     pivots = (pivot2, pivot1)
     panels = (panel2, panel1)
 
     def rows_of(group, index, way):
-        _, base, span, _ = groups[group]
+        _, base, span, cut, q, _ = groups[group]
         chunk = span // n
-        half = chunk // 2
-        return pl.ds(pl.multiple_of(base + (index % n) * chunk + way * half, 8), half)
+        size = chunk // 2 // cut
+        return pl.ds(pl.multiple_of(base + (index % n) * chunk + (way * cut + q) * size, 8), size)
 
     def ring_copy(group, way, step):
-        kind, _, _, slot = groups[group]
+        kind, _, _, _, _, slot = groups[group]
         sign = 1 - 2 * way
         if step < n - 1:
             if step == 0:
@@ -105,7 +110,7 @@
             pending.append(copy)
 
     def ring_step(group, step):
-        kind, _, _, slot = groups[group]
+        kind, _, _, _, _, slot = groups[group]
         for way in range(2):
             sign = 1 - 2 * way
             ring_copy(group, way, step).wait_recv()
@@ -124,10 +129,11 @@
     def block_of(k):
         return pl.ds(pl.multiple_of(k * BLOCK, BLOCK), BLOCK)
 
-    def products(kind, first, last):
+    def products(kind, first, last, start=0, count=blocks):
         @pl.loop(first, last)
         def _(k):
-            part[kind, block_of(k), :] = dot3(split(g[:, block_of(k)].T), split(rows[kind]))
+            where = block_of((start + k) % count)
+            part[kind, where, :] = dot3(split(g[:, where].T), split(rows[kind]))
 
     def lefts(kind, first, last):
         @pl.loop(first, last)
@@ -179,12 +185,18 @@
     last_block = early // BLOCK
     loads[0].wait()
     loads[1].wait()
-    products(0, 0, blocks)
+    first0 = pos * (width // n) // BLOCK
+    first1 = pos * (early // n) // BLOCK
+    products(0, 0, 2, first0)
     pl.semaphore_wait(barrier, m + 1)
-    ring_start(0)
+    for q in range(parts):
+        ring_start(2 * q)
     loads[2].wait()
-    products(1, 0, last_block)
-    ring_start(1)
+    products(1, 0, 2, first1, last_block)
+    for q in range(parts):
+        ring_start(2 * q + 1)
+    products(0, 2, blocks, first0)
+    products(1, 2, last_block, first1, last_block)
     loads[3].wait()
     lefts(0, 0, blocks)
     col_scatter(0)
@@ -193,18 +205,12 @@
     steps = 2 * n - 2
     late = 0
     for step in range(steps):
-        if step >= LATE:
-            for _ in range(2):
-                if late < steps:
-                    ring_step(2, late)
-                    late += 1
-                if _ == 0:
-                    ring_step(0, step)
-                else:
-                    ring_step(1, step)
-        else:
-            ring_step(0, step)
-            ring_step(1, step)
+        for kind in range(2):
+            if step >= LATE and late < steps:
+                ring_step(late_group, late)
+                late += 1
+            for q in range(parts):
+                ring_step(2 * q + kind, step)
         if step < 3:
             lefts(1, step * last_block // 3, (step + 1) * last_block // 3)
         if step == 2:
@@ -217,13 +223,13 @@
                 g[:, early:] += panel2[...]
 
             products(1, last_block, blocks)
-            ring_start(2)
+            ring_start(late_group)
             lefts(1, last_block, blocks)
             col_scatter(1)
         if step == LATE + 2:
             col_gather(1)
     while late < steps:
-        ring_step(2, late)
+        ring_step(late_group, late)
         late += 1
     col_finish(1)
 
@@ -254,6 +260,7 @@
         vmem = pl.BlockSpec(memory_space=pltpu.VMEM)
         shapes = ((height, nb), (width, nb), (height, nb), (width, nb))
         steps = 2 * n - 2
+        parts = 1 if any(w % (32 * n) for w in (width, width - nb)) else 2
         results = pl.pallas_call(
             functools.partial(kernel, n, m),
             out_shape=tuple(pltpu.VMEM(s, F32) for s in shapes),
@@ -265,21 +272,21 @@
                 pltpu.VMEM((2, width, nb), F32),
                 pltpu.VMEM((2, nb, nb), F32),
                 pltpu.VMEM((2, width, nb), F32),
-                pltpu.VMEM((2, n - 1, width // n // 2, nb), F32),
-                pltpu.VMEM((2, n - 1, (width - nb) // n // 2, nb), F32),
+                pltpu.VMEM((parts, 2, n - 1, width // n // 2 // parts, nb), F32),
+                pltpu.VMEM((parts, 2, n - 1, (width - nb) // n // 2 // parts, nb), F32),
                 pltpu.VMEM((2, n - 1, nb // n // 2, nb), F32),
                 pltpu.VMEM((2, height, nb), F32),
                 pltpu.VMEM((2, m - 1, height // m, nb), F32),
                 pltpu.SemaphoreType.DMA((7,)),
-                pltpu.SemaphoreType.DMA((3, 2, steps)),
-                pltpu.SemaphoreType.DMA((3, 2, steps)),
+                pltpu.SemaphoreType.DMA((2 * parts + 1, 2, steps)),
+                pltpu.SemaphoreType.DMA((2 * parts + 1, 2, steps)),
                 pltpu.SemaphoreType.DMA((2, 2, m - 1)),
                 pltpu.SemaphoreType.DMA((2, 2, m - 1)),
             ],
             compiler_params=pltpu.CompilerParams(
                 collective_id=0, has_side_effects=True, vmem_limit_bytes=VMEM_LIMIT
             ),
-        )(g, r1, c1, r2, c2, i1, i2)
+        )(*[pltpu.with_memory_space_constraint(x, pltpu.HBM) for x in (g, r1, c1, r2, c2, i1, i2)])
         return pl.pallas_call(
             write_out,
             out_shape=tuple(jax.ShapeDtypeStruct(s, F32) for s in shapes),

time: 93.3 us -> 90.3 us (0.968)
  local copies, waits for them, and re-layouts: 2.93 us -> 0 us
    unnamed x6 -> x0, local copies, waits for them, and re-layouts: 2.93 us -> none
where the time goes in v3:
time: 90.3 us; the launch traced here: 90.2 us
  Pallas kernels  89.5 us (99%)
    pallas_call x1, Pallas kernels, local(): pl.pallas_call(functools.partial(kernel, n, m), out_shape=tuple((pltpu.VM...  87.3 us
    pallas_call x1, Pallas kernels, local(): pl.pallas_call(write_out, out_shape=tuple((jax.ShapeDtypeStruct(s, F32) f...  2.21 us

profile of v3, /device:TPU:0, one launch (start us, length us, event | category | flops | bytes accessed | tf_op | source)
XLA Modules:
  0.0 90.2 jit_solution(3964387869481362601)
XLA Ops:
  0.6 87.3 %shard_map.102 = (f32[512,256]{1,0:T(8,128)S(1)}, f32[1792,256]{1,0:T(8,128)S(1)}, f32[512,256]{1,0:T(8,128)S(1)}, f32[1792,256]{1,0:T(8,128)S(1)}) custom-call(f32[512,1792]{1,0:T(8,128)} %g_hbm.1, f32[512,256]{1,0:T(8,128)} %r1_hbm.1, f32[1792,256]{1,0:T(8,128)} %c1_hbm.1, f32[512,256]{1,0:T(8,128)} %r2_hbm.1, f32[1792,256]{1,0:T(8,128)} %c2_hbm.1, ...), custom_call_target="tpu_custom_call" | custom-call | tf_op jit(solution)/shard_map/pallas_call | solution.py:264
  88.0 2.2 %shard_map.103 = (f32[512,256]{1,0:T(8,128)}, f32[1792,256]{1,0:T(8,128)}, f32[512,256]{1,0:T(8,128)}, f32[1792,256]{1,0:T(8,128)}) custom-call(f32[512,256]{1,0:T(8,128)S(1)} %get-tuple-element.8.refs_0_, f32[1792,256]{1,0:T(8,128)S(1)} %get-tuple-element.9.refs_1_, f32[512,256]{1,0:T(8,128)S(1)} %get-tuple-element.10.refs_2_, ...), custom_call_target="tpu_custom_call" | custom-call | tf_op jit(solution)/shard_map/pallas_call | solution.py:290

commit v4 on v3

--- a/solution.py
+++ b/solution.py
@@ -11,6 +11,7 @@
 F32 = jnp.float32
 BLOCK = 256
 LATE = 5
+PIECES = 4
 VMEM_LIMIT = 48 << 20
 
 
@@ -31,7 +32,7 @@
     g_hbm, r1_hbm, c1_hbm, r2_hbm, c2_hbm, i1_hbm, i2_hbm,
     panel2, pivot2, panel1, pivot1,
     g, rows, cols, inv, part, slot2, slot1, slot_late, left, gathered,
-    load_sem, ring_send, ring_recv, col_send, col_recv,
+    tile_sem, load_sem, ring_send, ring_recv, col_send, col_recv,
 ):
     height, width = g.shape
     nb = inv.shape[-1]
@@ -50,12 +51,25 @@
 
     following, preceding = at_position(pos + 1), at_position(pos + n - 1)
 
-    sources = (g_hbm, r2_hbm, r1_hbm, c2_hbm, i2_hbm, c1_hbm, i1_hbm)
-    targets = (g, rows.at[0], rows.at[1], cols.at[0], inv.at[0], cols.at[1], inv.at[1])
+    first0 = pos * (width // n) // BLOCK
+    first1 = pos * (early // n) // BLOCK
+
+    def block_of(k):
+        return pl.ds(pl.multiple_of(k * BLOCK, BLOCK), BLOCK)
+
+    def tile_load(k):
+        where = block_of((first0 + k) % blocks)
+        return pltpu.make_async_copy(g_hbm.at[:, where], g.at[:, where], tile_sem.at[k])
+
+    sources = (r2_hbm, r1_hbm, c2_hbm, i2_hbm, c1_hbm, i1_hbm)
+    targets = (rows.at[0], rows.at[1], cols.at[0], inv.at[0], cols.at[1], inv.at[1])
     loads = [
         pltpu.make_async_copy(s, t, load_sem.at[k]) for k, (s, t) in enumerate(zip(sources, targets))
     ]
-    for load in loads:
+    loads[0].start()
+    for k in range(blocks):
+        tile_load(k).start()
+    for load in loads[1:]:
         load.start()
 
     barrier = pltpu.get_barrier_semaphore()
@@ -126,9 +140,6 @@
                 copy.start()
                 pending.append(copy)
 
-    def block_of(k):
-        return pl.ds(pl.multiple_of(k * BLOCK, BLOCK), BLOCK)
-
     def products(kind, first, last, start=0, count=blocks):
         @pl.loop(first, last)
         def _(k):
@@ -184,23 +195,21 @@
     left[...] = jnp.zeros_like(left)
     last_block = early // BLOCK
     loads[0].wait()
-    loads[1].wait()
-    first0 = pos * (width // n) // BLOCK
-    first1 = pos * (early // n) // BLOCK
+    tile_load(0).wait()
+    tile_load(1).wait()
     products(0, 0, 2, first0)
     pl.semaphore_wait(barrier, m + 1)
     for q in range(parts):
         ring_start(2 * q)
-    loads[2].wait()
+    for k in range(2, blocks):
+        tile_load(k).wait()
+    loads[1].wait()
     products(1, 0, 2, first1, last_block)
     for q in range(parts):
         ring_start(2 * q + 1)
     products(0, 2, blocks, first0)
     products(1, 2, last_block, first1, last_block)
-    loads[3].wait()
-    lefts(0, 0, blocks)
-    col_scatter(0)
-    for load in loads[4:]:
+    for load in loads[2:]:
         load.wait()
     steps = 2 * n - 2
     late = 0
@@ -211,8 +220,12 @@
                 late += 1
             for q in range(parts):
                 ring_step(2 * q + kind, step)
-        if step < 3:
-            lefts(1, step * last_block // 3, (step + 1) * last_block // 3)
+            if step == 0:
+                lefts(0, kind * (blocks // 2), blocks if kind else blocks // 2)
+        if step == 0:
+            col_scatter(0)
+        elif step < 4:
+            lefts(1, (step - 1) * last_block // 3, step * last_block // 3)
         if step == 2:
             col_gather(0)
         if step == LATE - 1:
@@ -243,7 +256,12 @@
 
 def write_out(*refs):
     sems = refs[-1]
-    copies = [pltpu.make_async_copy(refs[k], refs[4 + k], sems.at[k]) for k in range(4)]
+    copies = []
+    for k in range(4):
+        size = refs[k].shape[0] // PIECES
+        for p in range(PIECES):
+            where = pl.ds(p * size, size)
+            copies.append(pltpu.make_async_copy(refs[k].at[where], refs[4 + k].at[where], sems.at[k, p]))
     for copy in copies:
         copy.start()
     for copy in copies:
@@ -277,7 +295,8 @@
                 pltpu.VMEM((2, n - 1, nb // n // 2, nb), F32),
                 pltpu.VMEM((2, height, nb), F32),
                 pltpu.VMEM((2, m - 1, height // m, nb), F32),
-                pltpu.SemaphoreType.DMA((7,)),
+                pltpu.SemaphoreType.DMA((width // BLOCK,)),
+                pltpu.SemaphoreType.DMA((6,)),
                 pltpu.SemaphoreType.DMA((2 * parts + 1, 2, steps)),
                 pltpu.SemaphoreType.DMA((2 * parts + 1, 2, steps)),
                 pltpu.SemaphoreType.DMA((2, 2, m - 1)),
@@ -292,7 +311,7 @@
             out_shape=tuple(jax.ShapeDtypeStruct(s, F32) for s in shapes),
             in_specs=[vmem] * 4,
             out_specs=(any_space,) * 4,
-            scratch_shapes=[pltpu.SemaphoreType.DMA((4,))],
+            scratch_shapes=[pltpu.SemaphoreType.DMA((4, PIECES))],
             compiler_params=pltpu.CompilerParams(vmem_limit_bytes=8 << 20),
         )(*results)
 

time: 90.3 us -> 88.2 us (0.977)
  Pallas kernels: 89.5 us -> 87.4 us
    pallas_call x1, Pallas kernels: 87.3 us -> 85.1 us  [local(): pl.pallas_call(functools.partial(kernel, n, m), out_shape=tuple((pltpu.VM...]
where the time goes in v4:
time: 88.2 us; the launch traced here: 88.1 us
  Pallas kernels  87.4 us (99%)
    pallas_call x1, Pallas kernels, local(): pl.pallas_call(functools.partial(kernel, n, m), out_shape=tuple((pltpu.VM...  85.1 us
    pallas_call x1, Pallas kernels, local(): pl.pallas_call(write_out, out_shape=tuple((jax.ShapeDtypeStruct(s, F32) f...  2.31 us

profile of v4, /device:TPU:0, one launch (start us, length us, event | category | flops | bytes accessed | tf_op | source)
XLA Modules:
  0.0 88.1 jit_solution(16783019189124840800)
XLA Ops:
  0.6 85.1 %shard_map.102 = (f32[512,256]{1,0:T(8,128)S(1)}, f32[1792,256]{1,0:T(8,128)S(1)}, f32[512,256]{1,0:T(8,128)S(1)}, f32[1792,256]{1,0:T(8,128)S(1)}) custom-call(f32[512,1792]{1,0:T(8,128)} %g_hbm.1, f32[512,256]{1,0:T(8,128)} %r1_hbm.1, f32[1792,256]{1,0:T(8,128)} %c1_hbm.1, f32[512,256]{1,0:T(8,128)} %r2_hbm.1, f32[1792,256]{1,0:T(8,128)} %c2_hbm.1, ...), custom_call_target="tpu_custom_call" | custom-call | tf_op jit(solution)/shard_map/pallas_call | solution.py:282
  85.7 2.3 %shard_map.103 = (f32[512,256]{1,0:T(8,128)}, f32[1792,256]{1,0:T(8,128)}, f32[512,256]{1,0:T(8,128)}, f32[1792,256]{1,0:T(8,128)}) custom-call(f32[512,256]{1,0:T(8,128)S(1)} %get-tuple-element.8.refs_0_, f32[1792,256]{1,0:T(8,128)S(1)} %get-tuple-element.9.refs_1_, f32[512,256]{1,0:T(8,128)S(1)} %get-tuple-element.10.refs_2_, ...), custom_call_target="tpu_custom_call" | custom-call | tf_op jit(solution)/shard_map/pallas_call | solution.py:309

commit v5 on v4

--- a/solution.py
+++ b/solution.py
@@ -10,7 +10,7 @@
 MESH = pl.DeviceIdType.MESH
 F32 = jnp.float32
 BLOCK = 256
-LATE = 5
+LATE = 6
 PIECES = 4
 VMEM_LIMIT = 48 << 20
 
@@ -226,7 +226,7 @@
             col_scatter(0)
         elif step < 4:
             lefts(1, (step - 1) * last_block // 3, step * last_block // 3)
-        if step == 2:
+        if step == 3:
             col_gather(0)
         if step == LATE - 1:
             col_finish(0)
@@ -278,7 +278,7 @@
         vmem = pl.BlockSpec(memory_space=pltpu.VMEM)
         shapes = ((height, nb), (width, nb), (height, nb), (width, nb))
         steps = 2 * n - 2
-        parts = 1 if any(w % (32 * n) for w in (width, width - nb)) else 2
+        parts = 1
         results = pl.pallas_call(
             functools.partial(kernel, n, m),
             out_shape=tuple(pltpu.VMEM(s, F32) for s in shapes),

time: 88.2 us -> 89.5 us (1.015)
  Pallas kernels: 87.4 us -> 88.7 us
    pallas_call x1, Pallas kernels: 85.1 us -> 86.4 us  [local(): pl.pallas_call(functools.partial(kernel, n, m), out_shape=tuple((pltpu.VM...]
where the time goes in v5:
time: 89.5 us; the launch traced here: 89.3 us
  Pallas kernels  88.7 us (99%)
    pallas_call x1, Pallas kernels, local(): pl.pallas_call(functools.partial(kernel, n, m), out_shape=tuple((pltpu.VM...  86.4 us
    pallas_call x1, Pallas kernels, local(): pl.pallas_call(write_out, out_shape=tuple((jax.ShapeDtypeStruct(s, F32) f...  2.31 us

profile of v5, /device:TPU:0, one launch (start us, length us, event | category | flops | bytes accessed | tf_op | source)
XLA Modules:
  0.0 89.3 jit_solution(3087101345519674929)
XLA Ops:
  0.6 86.4 %shard_map.102 = (f32[512,256]{1,0:T(8,128)S(1)}, f32[1792,256]{1,0:T(8,128)S(1)}, f32[512,256]{1,0:T(8,128)S(1)}, f32[1792,256]{1,0:T(8,128)S(1)}) custom-call(f32[512,1792]{1,0:T(8,128)} %g_hbm.1, f32[512,256]{1,0:T(8,128)} %r1_hbm.1, f32[1792,256]{1,0:T(8,128)} %c1_hbm.1, f32[512,256]{1,0:T(8,128)} %r2_hbm.1, f32[1792,256]{1,0:T(8,128)} %c2_hbm.1, ...), custom_call_target="tpu_custom_call" | custom-call | tf_op jit(solution)/shard_map/pallas_call | solution.py:282
  87.0 2.3 %shard_map.103 = (f32[512,256]{1,0:T(8,128)}, f32[1792,256]{1,0:T(8,128)}, f32[512,256]{1,0:T(8,128)}, f32[1792,256]{1,0:T(8,128)}) custom-call(f32[512,256]{1,0:T(8,128)S(1)} %get-tuple-element.8.refs_0_, f32[1792,256]{1,0:T(8,128)S(1)} %get-tuple-element.9.refs_1_, f32[512,256]{1,0:T(8,128)S(1)} %get-tuple-element.10.refs_2_, ...), custom_call_target="tpu_custom_call" | custom-call | tf_op jit(solution)/shard_map/pallas_call | solution.py:309
